TPU v7x, 32 devices: a whole 2x2x4 slice. The times are simulated.
32 devices in a mesh: subj: 2 (over x), row: 8 (over z, y), col: 2 (over core).
Axes of the slice: x: 2, y: 2, z: 4, core: 2. Of those that a mesh axis runs over, the one named last changes fastest.
Arguments:
- bold: bfloat16 [4, 256, 16, 16, 128], P('subj', None, 'row', 'col'), parts along dimension 0, may hold values from -6 to 6
- gm_index: int32 [16384], P(('row', 'col')), may hold values from -1 to 2047, as said below
- partners: int32 [128, 16], P(('row', 'col')), may hold values from -1 to 127, as said below
Outputs:
- connectome: bfloat16 [128, 16, 4, 128, 128], P(('row', 'col'), None, 'subj'), parts along dimension 2
There are 2 independent parts, one for each index of `subj`. A program takes and returns all parts, laid end to end along the dimension named above; an argument that names none is the same for every part. Nothing has to cross between parts.
Inputs may be any that keep to these rules, and one draw needn't show every extreme that they name: `gm_index`: entries of one slab's 1024 rows are distinct voxel numbers, the last few of them -1; every slab has some -1 rows. `partners`: block g lies in slab g // 8, slabs numbered row-major over slab rows and columns. Slot 0 of block i names i, slot 1 names (i + 1) mod 128, slot 2 names (i - 1) mod 128; every named block lies in a slab whose slab row is within 2 of block i's slab row, counted cyclically. -1 marks an empty slot.
All inputs are finite; a program needn't handle non-finite values.
Results may differ from a plain program's by a relative error of at most 0.0053.
Values may be sent and summed in bfloat16 or wider, within the bound.
A program may use at most 128 MiB of HBM per device.

v0:
```python
import math

import jax
import jax.numpy as jnp
from jax import lax
from jax.sharding import PartitionSpec as P

HOP = 2


side_weight = math.exp(-0.5) / (1.0 + 2.0 * math.exp(-0.5))
centre_weight = 1.0 / (1.0 + 2.0 * math.exp(-0.5))


def from_behind(value, axis, steps):
    count = lax.axis_size(axis)
    pairs = [(source, (source + steps) % count) for source in range(count)]
    return lax.ppermute(value, axis, pairs)


def padded_2(block, sides, width):
    for axis, dim in sides:
        count = lax.axis_size(axis)
        forward = [(i, i + 1) for i in range(count - 1)]
        backward = [(target, source) for source, target in forward]
        low = lax.ppermute(
            lax.slice_in_dim(block, block.shape[dim] - width, None, axis=dim), axis, forward
        )
        high = lax.ppermute(lax.slice_in_dim(block, 0, width, axis=dim), axis, backward)
        block = jnp.concatenate([low, block, high], axis=dim)
    return block


def gaussian_blur(padded):
    first = (
        side_weight * padded[:, :, :-2]
        + centre_weight * padded[:, :, 1:-1]
        + side_weight * padded[:, :, 2:]
    )
    second = (
        side_weight * first[:, :, :, :-2]
        + centre_weight * first[:, :, :, 1:-1]
        + side_weight * first[:, :, :, 2:]
    )
    return (
        side_weight * second[..., :-2]
        + centre_weight * second[..., 1:-1]
        + side_weight * second[..., 2:]
    )


def standardize(smooth):
    windows, frames = (smooth.shape[0], smooth.shape[1])
    series = smooth.reshape(windows, frames, -1)
    centred = series - jnp.mean(series, axis=1, keepdims=True)
    spread = jnp.mean(centred * centred, axis=1, keepdims=True)
    scored = centred * lax.rsqrt((spread + 1e-05) * frames)
    return jnp.transpose(scored, (2, 0, 1)).astype(jnp.bfloat16)


def nearby_rows(source):
    lower_rows = []
    current = source
    for hop_step in range(HOP):
        current = from_behind(current, "row", 1)
        lower_rows.append(current)
    upper_rows = []
    current = source
    for hop_step in range(HOP):
        current = from_behind(current, "row", -1)
        upper_rows.append(current)
    ordered = lower_rows[::-1] + [source] + upper_rows
    return jnp.stack(ordered, 0)


def on_device(bold, gm_index, partners):
    padded = padded_2(bold, (("row", 2), ("col", 3)), 1)
    widened = jnp.pad(padded.astype(jnp.float32), ((0, 0), (0, 0), (0, 0), (0, 0), (1, 1)))
    scored = standardize(gaussian_blur(widened))
    picked = jnp.take(scored, jnp.maximum(gm_index, 0), axis=0)
    panel = jnp.where((gm_index >= 0)[:, None, None], picked, jnp.zeros_like(picked))
    row_count, windows, frames = panel.shape
    block_count = partners.shape[0]
    block_rows = row_count // block_count
    flat_panel = panel.reshape(row_count, windows * frames)
    col_count = lax.axis_size("col")
    own_column = nearby_rows(flat_panel)
    collected = lax.all_gather(own_column, "col", axis=1, tiled=True)
    candidates = collected.reshape(
        (2 * HOP + 1) * col_count * block_count, block_rows, windows, frames
    )
    row_here = lax.axis_index("row")
    row_total = lax.axis_size("row")
    partner_ids = jnp.maximum(partners, 0)
    source_slab = partner_ids // block_count
    distance_slot = (source_slab // col_count - row_here + HOP + row_total) % row_total
    position = (
        distance_slot * col_count + source_slab % col_count
    ) * block_count + partner_ids % block_count
    local_blocks = panel.reshape(block_count, block_rows, windows, frames)

    def block_tiles(inputs):
        local_block, where_from, present = inputs
        partner_rows = jnp.take(candidates, where_from, axis=0)
        tiles_out = jnp.einsum(
            "awf,kbwf->kwab", local_block, partner_rows, preferred_element_type=jnp.float32
        )
        tiles_out = jnp.where(present[:, None, None, None], tiles_out, jnp.zeros_like(tiles_out))
        return tiles_out.astype(jnp.bfloat16)

    return lax.map(block_tiles, (local_blocks, position, partners >= 0))


def solution(mesh):
    in_specs = (P("subj", None, "row", "col", None), P(("row", "col")), P(("row", "col"), None))
    out_specs = P(("row", "col"), None, "subj", None, None)
    return jax.shard_map(
        on_device, mesh=mesh, in_specs=in_specs, out_specs=out_specs, check_vma=False
    )
```

profile of v0, /device:TPU:0, one launch (start us, length us, event | category | flops | bytes accessed | tf_op | source)
XLA Modules:
  0.0 382.9 jit_solution(14022659666264512104)
XLA Ops:
  8.6 5.0 %collective-permute-start = (bf16[2,256,1,8,128]{4,1,3,2,0:T(8,128)(2,1)S(1)}, bf16[2,256,1,8,128]{4,1,3,2,0:T(8,128)(2,1)S(1)}, u32[]{:S(2)}, u32[]{:S(2)}) collective-permute-start(bf16[2,256,1,8,128]{4,1,3,2,0:T(8,128)(2,1)S(1)} %copy.38), channel_id=1, source_target_pairs={{0,2},{2,4},{4,6},{6,8},{8,10},{10,12},{12,14},{1,3},{3,5},{5,7},{... | collective-permute-start | bytes 3145736 | tf_op jit(solution)/shard_map/ppermute | solution.py:26
  15.0 43.3 %collective-permute-done = bf16[2,256,1,8,128]{4,1,3,2,0:T(8,128)(2,1)S(1)} collective-permute-done((bf16[2,256,1,8,128]{4,1,3,2,0:T(8,128)(2,1)S(1)}, bf16[2,256,1,8,128]{4,1,3,2,0:T(8,128)(2,1)S(1)}, u32[]{:S(2)}, u32[]{:S(2)}) %collective-permute-start) | collective-permute-done | bytes 1048608 | tf_op jit(solution)/shard_map/ppermute | solution.py:26
  64.5 6.6 %fusion.17 = f32[2,256,4,10,130]{4,1,3,2,0:T(8,128)S(1)} fusion(bf16[2,256,4,1,128]{4,1,3,2,0:T(8,128)(2,1)S(1)} %collective-permute-done.3, bf16[2,256,4,8,128]{4,1,3,2,0:T(8,128)(2,1)S(1)} %constant_dynamic-update-slice_fusion.1, bf16[2,256,4,1,128]{4,1,3,2,0:T(8,128)(2,1)S(1)} %collective-permute-done.2), kind=kLoop, calls=%fused_computation.26 | loop fusion | flops 31948800 | bytes 15892480 | tf_op jit(solution)/shard_map/jit(_pad)/pad | solution.py:78
  71.1 6.1 %fusion.18 = f32[2,256,2,10,130]{4,1,3,2,0:T(8,128)} fusion(f32[2,256,4,10,130]{4,1,3,2,0:T(8,128)S(1)} %fusion.17), kind=kLoop, calls=%fused_computation.28 | loop fusion | flops 6656000 | bytes 21299200 | tf_op jit(solution)/shard_map/add | solution.py:36
  77.2 9.6 %fusion.20 = f32[2,256,2,8,130]{4,1,3,2,0:T(8,128)S(1)} fusion(f32[2,256,2,10,130]{4,1,3,2,0:T(8,128)} %fusion.18), kind=kLoop, calls=%fused_computation.33 | loop fusion | flops 5324800 | bytes 17039360 | tf_op jit(solution)/shard_map/add | solution.py:41
  86.9 3.7 fusion.35
  90.5 7.3 %copy.19 = f32[2,256,2,8,128]{1,0,4,3,2:T(2,128)} copy(f32[2,256,2,8,128]{4,1,3,2,0:T(8,128)} %get-tuple-element.63) | data formatting | bytes 8388608 | tf_op jit(solution)/shard_map/add | solution.py:46
  97.8 2.8 multiply_reduce_fusion
  102.3 10.4 %fusion.25 = bf16[2,256,2048]{1,0,2:T(2,128)(2,1)S(1)} fusion(f32[2,256,2,8,128]{1,0,4,3,2:T(2,128)} %copy.19, f32[2,2048]{0,1:T(8,128)} %bitcast.59, f32[2,2048]{0,1:T(8,128)S(1)} %bitcast.58), kind=kLoop, calls=%fused_computation.44 | loop fusion | flops 3145728 | bytes 6324224 | tf_op jit(solution)/shard_map/convert_element_type | solution.py:58
  112.7 4.2 %gather_fusion.1 = bf16[1024,2,256]{2,1,0:T(2,128)(2,1)S(1)} fusion(bf16[2048,2,256]{2,1,0:T(2,128)(2,1)S(1)} %bitcast.55, s32[1024]{0:T(1024)S(1)} %maximum_clamp_fusion), kind=kCustom, calls=%fused_computation.1 | custom fusion | bytes 2101248 | tf_op jit(solution)/shard_map/jit(_take)/gather | solution.py:80
  122.7 42.9 %collective-permute-done.4 = bf16[1024,512]{1,0:T(8,128)(2,1)} collective-permute-done((bf16[1024,512]{1,0:T(8,128)(2,1)S(1)}, bf16[1024,512]{1,0:T(8,128)(2,1)}, u32[]{:S(2)}, u32[]{:S(2)}) %collective-permute-start.4) | collective-permute-done | bytes 1048608 | tf_op jit(solution)/shard_map/ppermute | solution.py:18
  169.0 2.8 collective-permute-start.7
  171.8 41.2 %collective-permute-done.5 = bf16[1024,512]{1,0:T(8,128)(2,1)} collective-permute-done((bf16[1024,512]{1,0:T(8,128)(2,1)}, bf16[1024,512]{1,0:T(8,128)(2,1)}, u32[]{:S(2)}, u32[]{:S(2)}) %collective-permute-start.5) | collective-permute-done | bytes 1048608 | tf_op jit(solution)/shard_map/ppermute | solution.py:18
  223.1 24.1 %all-gather.2.cloned.1.call-done = bf16[5,2048,512]{2,1,0:T(8,128)(2,1)} async-done(((bf16[5,1024,512]{2,1,0:T(8,128)(2,1)}), bf16[5,2048,512]{2,1,0:T(8,128)(2,1)}) %all-gather.2.cloned.1.call-update) | async-done | bytes 10485776 | tf_op jit(solution)/shard_map/all_gather | solution.py:88
  247.3 15.3 %reshape.127 = bf16[80,128,2,256]{3,2,1,0:T(2,128)(2,1)} reshape(bf16[5,2048,512]{2,1,0:T(8,128)(2,1)} %all-gather.2.cloned.1.call-done) | data formatting | bytes 20971520 | tf_op jit(solution)/shard_map/reshape | solution.py:89
  262.6 113.4 %while.10 = (s32[]{:T(128)}, bf16[8,16,2,128,128]{4,3,2,1,0:T(8,128)(2,1)}, pred[8,16]{1,0:T(8,128)(4,1)S(1)}, s32[8,16]{1,0:T(8,128)S(1)}, bf16[80,128,2,256]{3...) while((s32[]{:T(128)}, bf16[8,16,2,128,128]{4,3,2,1,0:T(8,128)(2,1)}, ...), condition=%wide.region_3.4_spmd, body=%wide.region_2.3_spmd.sunk | while | flops 270533792 | bytes 15865309 | solution.py:111
  262.6 9.8 %gather_fusion = bf16[16,128,2,256]{3,2,1,0:T(2,128)(2,1)S(1)} fusion(bf16[80,128,2,256]{3,2,1,0:T(2,128)(2,1)} %get-tuple-element.125, s32[1024]{0:T(1024)S(1)} %pad_clamp_fusion.2), kind=kCustom, calls=%fused_computation.clone.1 | custom fusion | bytes 4194368 | tf_op jit(solution)/shard_map/while/body/eval_jaxpr/jit(_take)/gather | solution.py:104
  276.8 9.8 %gather_fusion = bf16[16,128,2,256]{3,2,1,0:T(2,128)(2,1)S(1)} fusion(bf16[80,128,2,256]{3,2,1,0:T(2,128)(2,1)} %get-tuple-element.125, s32[1024]{0:T(1024)S(1)} %pad_clamp_fusion.2), kind=kCustom, calls=%fused_computation.clone.1 | custom fusion | bytes 4194368 | tf_op jit(solution)/shard_map/while/body/eval_jaxpr/jit(_take)/gather | solution.py:104
  291.0 9.8 %gather_fusion = bf16[16,128,2,256]{3,2,1,0:T(2,128)(2,1)S(1)} fusion(bf16[80,128,2,256]{3,2,1,0:T(2,128)(2,1)} %get-tuple-element.125, s32[1024]{0:T(1024)S(1)} %pad_clamp_fusion.2), kind=kCustom, calls=%fused_computation.clone.1 | custom fusion | bytes 4194368 | tf_op jit(solution)/shard_map/while/body/eval_jaxpr/jit(_take)/gather | solution.py:104
  305.2 9.8 %gather_fusion = bf16[16,128,2,256]{3,2,1,0:T(2,128)(2,1)S(1)} fusion(bf16[80,128,2,256]{3,2,1,0:T(2,128)(2,1)} %get-tuple-element.125, s32[1024]{0:T(1024)S(1)} %pad_clamp_fusion.2), kind=kCustom, calls=%fused_computation.clone.1 | custom fusion | bytes 4194368 | tf_op jit(solution)/shard_map/while/body/eval_jaxpr/jit(_take)/gather | solution.py:104
  319.3 9.8 %gather_fusion = bf16[16,128,2,256]{3,2,1,0:T(2,128)(2,1)S(1)} fusion(bf16[80,128,2,256]{3,2,1,0:T(2,128)(2,1)} %get-tuple-element.125, s32[1024]{0:T(1024)S(1)} %pad_clamp_fusion.2), kind=kCustom, calls=%fused_computation.clone.1 | custom fusion | bytes 4194368 | tf_op jit(solution)/shard_map/while/body/eval_jaxpr/jit(_take)/gather | solution.py:104
  333.5 9.8 %gather_fusion = bf16[16,128,2,256]{3,2,1,0:T(2,128)(2,1)S(1)} fusion(bf16[80,128,2,256]{3,2,1,0:T(2,128)(2,1)} %get-tuple-element.125, s32[1024]{0:T(1024)S(1)} %pad_clamp_fusion.2), kind=kCustom, calls=%fused_computation.clone.1 | custom fusion | bytes 4194368 | tf_op jit(solution)/shard_map/while/body/eval_jaxpr/jit(_take)/gather | solution.py:104
  347.7 9.8 %gather_fusion = bf16[16,128,2,256]{3,2,1,0:T(2,128)(2,1)S(1)} fusion(bf16[80,128,2,256]{3,2,1,0:T(2,128)(2,1)} %get-tuple-element.125, s32[1024]{0:T(1024)S(1)} %pad_clamp_fusion.2), kind=kCustom, calls=%fused_computation.clone.1 | custom fusion | bytes 4194368 | tf_op jit(solution)/shard_map/while/body/eval_jaxpr/jit(_take)/gather | solution.py:104
  361.8 9.8 %gather_fusion = bf16[16,128,2,256]{3,2,1,0:T(2,128)(2,1)S(1)} fusion(bf16[80,128,2,256]{3,2,1,0:T(2,128)(2,1)} %get-tuple-element.125, s32[1024]{0:T(1024)S(1)} %pad_clamp_fusion.2), kind=kCustom, calls=%fused_computation.clone.1 | custom fusion | bytes 4194368 | tf_op jit(solution)/shard_map/while/body/eval_jaxpr/jit(_take)/gather | solution.py:104
  (109 shorter events, 65.4 us)
Async XLA Ops:
  6.5 51.9 %copy-start = (bf16[2,256,2,8,128]{4,3,2,1,0:T(8,128)(2,1)S(1)}, bf16[2,256,2,8,128]{4,3,2,1,0:T(8,128)(2,1)}, u32[]{:S(2)}) copy-start(bf16[2,256,2,8,128]{4,3,2,1,0:T(8,128)(2,1)} %param.5) | copy-start | bytes 6291460
  6.5 240.7 %all-gather.2.cloned.1.call-start = ((), (), s32[]{:S(2)}) async-start(), calls=%async_computation | async-start | bytes 15728640 | tf_op jit(solution)/shard_map/all_gather | solution.py:88
  8.6 49.8 %collective-permute-start = (bf16[2,256,1,8,128]{4,1,3,2,0:T(8,128)(2,1)S(1)}, bf16[2,256,1,8,128]{4,1,3,2,0:T(8,128)(2,1)S(1)}, u32[]{:S(2)}, u32[]{:S(2)}) collective-permute-start(bf16[2,256,1,8,128]{4,1,3,2,0:T(8,128)(2,1)S(1)} %copy.38), channel_id=1, source_target_pairs={{0,2},{2,4},{4,6},{6,8},{8,10},{10,12},{12,14},{1,3},{3,5},{5,7},{... | collective-permute-start | bytes 3145736 | tf_op jit(solution)/shard_map/ppermute | solution.py:26
  13.7 48.3 %copy-start.2 = (s32[1024]{0:T(1024)S(1)}, s32[1024]{0:T(1024)}, u32[]{:S(2)}) copy-start(s32[1024]{0:T(1024)} %param.6) | copy-start | bytes 12292
  13.7 45.4 %collective-permute-start.1 = (bf16[2,256,1,8,128]{4,1,3,2,0:T(8,128)(2,1)S(1)}, bf16[2,256,1,8,128]{4,1,3,2,0:T(8,128)(2,1)S(1)}, u32[]{:S(2)}, u32[]{:S(2)}) collective-permute-start(bf16[2,256,1,8,128]{4,1,3,2,0:T(8,128)(2,1)S(1)} %copy.39), channel_id=1, source_target_pairs={{2,0},{4,2},{6,4},{8,6},{10,8},{12,10},{14,12},{3,1},{5,3},{7,5},{... | collective-permute-start | bytes 3145736 | tf_op jit(solution)/shard_map/ppermute | solution.py:29
  59.4 2.8 collective-permute-start.2
  60.7 3.8 collective-permute-start.3
  117.9 47.7 %collective-permute-start.4 = (bf16[1024,512]{1,0:T(8,128)(2,1)S(1)}, bf16[1024,512]{1,0:T(8,128)(2,1)}, u32[]{:S(2)}, u32[]{:S(2)}) collective-permute-start(bf16[1024,512]{1,0:T(8,128)(2,1)S(1)} %select_select_fusion.1), channel_id=1, source_target_pairs={{0,2},{2,4},{4,6},{6,8},{8,10},{10,12},{12,14},{14,0},{1,3},{3,5},... | collective-permute-start | bytes 3145736 | tf_op jit(solution)/shard_map/ppermute | solution.py:18
  120.5 48.5 %collective-permute-start.6 = (bf16[1024,512]{1,0:T(8,128)(2,1)S(1)}, bf16[1024,512]{1,0:T(8,128)(2,1)}, u32[]{:S(2)}, u32[]{:S(2)}) collective-permute-start(bf16[1024,512]{1,0:T(8,128)(2,1)S(1)} %select_select_fusion.1), channel_id=1, source_target_pairs={{0,14},{2,0},{4,2},{6,4},{8,6},{10,8},{12,10},{14,12},{1,15},{3,1}... | collective-permute-start | bytes 3145736 | tf_op jit(solution)/shard_map/ppermute | solution.py:18
  165.7 47.2 %collective-permute-start.5 = (bf16[1024,512]{1,0:T(8,128)(2,1)}, bf16[1024,512]{1,0:T(8,128)(2,1)}, u32[]{:S(2)}, u32[]{:S(2)}) collective-permute-start(bf16[1024,512]{1,0:T(8,128)(2,1)} %collective-permute-done.4), channel_id=1, source_target_pairs={{0,2},{2,4},{4,6},{6,8},{8,10},{10,12},{12,14},{14,0},{1,3},{3,5},... | collective-permute-start | bytes 3145736 | tf_op jit(solution)/shard_map/ppermute | solution.py:18
  169.0 52.4 %collective-permute-start.7 = (bf16[1024,512]{1,0:T(8,128)(2,1)}, bf16[1024,512]{1,0:T(8,128)(2,1)S(1)}, u32[]{:S(2)}, u32[]{:S(2)}) collective-permute-start(bf16[1024,512]{1,0:T(8,128)(2,1)} %collective-permute-done.6), channel_id=1, source_target_pairs={{0,14},{2,0},{4,2},{6,4},{8,6},{10,8},{12,10},{14,12},{1,15},{3,1}... | collective-permute-start | bytes 3145736 | tf_op jit(solution)/shard_map/ppermute | solution.py:18
  219.1 3.4 copy-start.1
Sparse Core Ops, SparseCore 0:
  222.6 24.6 all-gather.1
where the time goes:
time: 384 us; the launch traced here: 383 us
  waiting for transfers between devices  154 us (40%)
  local copies, waits for them, and re-layouts  133 us (35%)
  other arithmetic  57.5 us (15%)
  starting transfers between devices  19 us (5%)
  between operations  13.7 us (4%)
  matrix products  5.71 us (1%)
    ppermute x4, waiting for transfers between devices, from_behind(): return lax.ppermute(value, axis, pairs)  84.1 us
    gather x8, local copies, waits for them, and re-layouts, block_tiles(): partner_rows = jnp.take(candidates, where_from, axis=0)  78.3 us
    ppermute x2, waiting for transfers between devices, padded_2(): lax.ppermute(lax.slice_in_dim(block, block.shape[dim] - width, None, axis...  43.4 us
    all_gather x1, waiting for transfers between devices, on_device(): collected = lax.all_gather(own_column, 'col', axis=1, tiled=True)  24.1 us
    reshape x1, local copies, waits for them, and re-layouts, on_device(): collected.reshape((2 * HOP + 1) * col_count * block_count, block_rows, wi...  15.3 us
    select_n x16, other arithmetic, block_tiles(): partner_rows = jnp.take(candidates, where_from, axis=0)  15.1 us
    dynamic_update_slice x16, local copies, waits for them, and re-layouts, on_device(): return lax.map(block_tiles, (local_blocks, position, partners >= 0))  13.7 us
    convert_element_type x1, other arithmetic, standardize(): return jnp.transpose(scored, (2, 0, 1)).astype(jnp.bfloat16)  10.4 us
  transfers between devices with their start and end apart: 9, of which 6 were waited for; matrix products, arithmetic and copies ran while one was open for 3% of the time, Pallas kernels for 0%

commit v1 on v0

v1 whole, which is shorter than its diff:
```python
import functools
import math

import jax
import jax.numpy as jnp
from jax import lax
from jax.experimental import pallas as pl
from jax.experimental.pallas import tpu as pltpu
from jax.sharding import PartitionSpec as P

HOP = 2
MESH = pl.DeviceIdType.MESH

side_weight = math.exp(-0.5) / (1.0 + 2.0 * math.exp(-0.5))
centre_weight = 1.0 / (1.0 + 2.0 * math.exp(-0.5))


def three(low, mid, high):
    return side_weight * low + centre_weight * mid + side_weight * high


def panel_kernel(
    rows,
    gm_ref,
    bold_ref,
    cand_ref,
    halo_lo,
    halo_hi,
    pick,
    xf,
    face_out,
    face_in,
    scored,
    panel,
    halo_send,
    halo_recv,
    face_send,
    face_recv,
    own_sem,
    panel_send,
    panel_recv,
):
    windows, frames, sx, sy, sz = bold_ref.shape
    voxels = sx * sy * sz
    count = gm_ref.shape[1]
    blocks = panel.shape[1]
    r = lax.axis_index("row")
    c = lax.axis_index("col")
    odd = lax.rem(r, 2)
    pair = r + 1 - 2 * odd
    up1 = lax.rem(r + 1, rows)
    down1 = lax.rem(r + rows - 1, rows)
    up2 = lax.rem(r + 2, rows)
    down2 = lax.rem(r + rows - 2, rows)
    other = {"col": 1 - c}

    barrier = pltpu.get_barrier_semaphore()
    pl.semaphore_signal(barrier, inc=1, device_id=other, device_id_type=MESH)
    for target in (up1, down1, up2, down2):
        pl.semaphore_signal(barrier, inc=1, device_id={"row": target}, device_id_type=MESH)
    pl.semaphore_wait(barrier, 5)

    def halo_up(w):
        return pltpu.make_async_remote_copy(
            src_ref=bold_ref.at[w, :, sx - 1],
            dst_ref=halo_lo.at[w],
            send_sem=halo_send.at[w, 0],
            recv_sem=halo_recv.at[w, 0],
            device_id={"row": up1},
            device_id_type=MESH,
        )

    def halo_down(w):
        return pltpu.make_async_remote_copy(
            src_ref=bold_ref.at[w, :, 0],
            dst_ref=halo_hi.at[w],
            send_sem=halo_send.at[w, 1],
            recv_sem=halo_recv.at[w, 1],
            device_id={"row": down1},
            device_id_type=MESH,
        )

    for w in range(windows):

        @pl.when(r < rows - 1)
        def _():
            halo_up(w).start()

        @pl.when(r > 0)
        def _():
            halo_down(w).start()

    @pl.when(r == 0)
    def _():
        halo_lo[...] = jnp.zeros_like(halo_lo)

    @pl.when(r == rows - 1)
    def _():
        halo_hi[...] = jnp.zeros_like(halo_hi)

    gm = gm_ref[...]

    def fill(step, carry):
        start = pl.multiple_of(step * sz, sz)
        ids = lax.broadcasted_iota(jnp.int32, (sz, count), 0) + start
        pick[pl.ds(start, sz), :] = (ids == gm).astype(jnp.float32).astype(jnp.bfloat16)
        return carry

    lax.fori_loop(0, voxels // sz, fill, 0)

    def send(w, src, slot, sem, target):
        return pltpu.make_async_remote_copy(
            src_ref=src,
            dst_ref=cand_ref.at[slot, w],
            send_sem=panel_send.at[w, sem],
            recv_sem=panel_recv.at[w, slot],
            device_id=target,
            device_id_type=MESH,
        )

    def own(w):
        return pltpu.make_async_copy(panel.at[w], cand_ref.at[2 * HOP + c, w], own_sem.at[w])

    def to_other(w):
        return send(w, panel.at[w], 2 * HOP + c, 0, other)

    def to_up2(w):
        return send(w, panel.at[w], c, 1, {"row": up2})

    def to_down2(w):
        return send(w, panel.at[w], 8 + c, 2, {"row": down2})

    def to_pair(w):
        return send(w, panel.at[w], 2 * (1 + 2 * odd) + c, 3, {"row": pair})

    def relay(w):
        mine = 2 * (4 - 4 * odd) + c
        return send(w, cand_ref.at[mine, w], 2 * (3 - 2 * odd) + c, 4, {"row": pair})

    def across(w, which, slot):
        return send(w, cand_ref.at[slot, w], slot, 5 + which, other)

    def arrived(w, slot):
        pltpu.make_async_remote_copy(
            src_ref=cand_ref.at[slot, w],
            dst_ref=cand_ref.at[slot, w],
            send_sem=panel_send.at[w, 0],
            recv_sem=panel_recv.at[w, slot],
            device_id=other,
            device_id_type=MESH,
        ).wait_recv()

    lane = lax.broadcasted_iota(jnp.int32, (1, sz), 1)
    first_lane = lane == 0
    last_lane = lane == sz - 1

    for w in range(windows):

        @pl.when(r > 0)
        def _():
            halo_up(w).wait_recv()

        @pl.when(r < rows - 1)
        def _():
            halo_down(w).wait_recv()

        chunk = 32

        def filter_x(step, carry):
            at = step * chunk
            here = pl.ds(at, chunk)
            low = halo_lo[w, here].astype(jnp.float32)
            first = bold_ref[w, here, 0].astype(jnp.float32)
            second = bold_ref[w, here, 1].astype(jnp.float32)
            high = halo_hi[w, here].astype(jnp.float32)
            flat = pl.ds(pl.multiple_of(at * sy, sy), chunk * sy)
            xf[0, flat, :] = three(low, first, second).reshape(chunk * sy, sz)
            xf[1, flat, :] = three(first, second, high).reshape(chunk * sy, sz)
            return carry

        lax.fori_loop(0, frames // chunk, filter_x, 0)

        for x in range(sx):

            @pl.when(c == 0)
            def _():
                face_out[w, x] = xf[x, pl.ds(sy - 1, frames, stride=sy), :]

            @pl.when(c == 1)
            def _():
                face_out[w, x] = xf[x, pl.ds(0, frames, stride=sy), :]

        face = pltpu.make_async_remote_copy(
            src_ref=face_out.at[w],
            dst_ref=face_in.at[w],
            send_sem=face_send.at[w],
            recv_sem=face_recv.at[w],
            device_id=other,
            device_id_type=MESH,
        )
        face.start()

        def row_of(x, y):
            return xf[x, pl.ds(y, frames, stride=sy), :]

        def finish(x, y, low, mid, high):
            plane = three(low, mid, high)
            left = jnp.where(first_lane, 0.0, pltpu.roll(plane, 1, 1))
            right = jnp.where(last_lane, 0.0, pltpu.roll(plane, sz - 1, 1))
            smooth = three(left, plane, right)
            centred = smooth - jnp.mean(smooth, axis=0, keepdims=True)
            spread = jnp.mean(centred * centred, axis=0, keepdims=True)
            value = centred * lax.rsqrt((spread + 1e-05) * frames)
            at = (x * sy + y) * sz
            scored[:, at : at + sz] = value.astype(jnp.bfloat16)

        for x in range(sx):
            for y in range(1, sy - 1):
                finish(x, y, row_of(x, y - 1), row_of(x, y), row_of(x, y + 1))
        face.wait()
        for x in range(sx):
            edge = face_in[w, x]
            nothing = jnp.zeros_like(edge)
            finish(x, 0, jnp.where(c == 1, edge, nothing), row_of(x, 0), row_of(x, 1))
            finish(x, sy - 1, row_of(x, sy - 2), row_of(x, sy - 1), jnp.where(c == 0, edge, nothing))

        wide = 2 * sz
        for piece in range(count // wide):
            got = jnp.dot(
                scored[...],
                pick[:, piece * wide : (piece + 1) * wide],
                preferred_element_type=jnp.float32,
            ).astype(jnp.bfloat16)
            panel[w, 2 * piece] = got[:, :sz]
            panel[w, 2 * piece + 1] = got[:, sz:]

        to_up2(w).start()
        to_down2(w).start()
        to_pair(w).start()
        to_other(w).start()
        own(w).start()

    order = (
        2 * (3 - 2 * odd) + c,
        2 * (4 - 4 * odd) + c,
        2 * (4 * odd) + c,
        2 * (1 + 2 * odd) + c,
    )
    for w in range(windows):
        arrived(w, order[0])
        across(w, 0, order[0]).start()
        arrived(w, order[1])
        relay(w).start()
        across(w, 1, order[1]).start()
        arrived(w, order[2])
        across(w, 2, order[2]).start()
    for w in range(windows):
        arrived(w, order[3])
        across(w, 3, order[3]).start()

    for w in range(windows):
        for slot in range(2 * HOP + 1):
            arrived(w, 2 * slot + 1 - c)

    for w in range(windows):

        @pl.when(r < rows - 1)
        def _():
            halo_up(w).wait_send()

        @pl.when(r > 0)
        def _():
            halo_down(w).wait_send()

        own(w).wait()
        to_other(w).wait_send()
        to_up2(w).wait_send()
        to_down2(w).wait_send()
        to_pair(w).wait_send()
        relay(w).wait_send()
        for which in range(4):
            across(w, which, order[which]).wait_send()


def tile_kernel(rows, cols, partners_ref, cand_ref, out_ref):
    i = pl.program_id(0)
    blocks = cand_ref.shape[2]
    block_rows = cand_ref.shape[4]
    windows = cand_ref.shape[1]
    slots = out_ref.shape[1]
    r = lax.axis_index("row")
    c = lax.axis_index("col")
    local = [cand_ref[HOP * cols + c, w, i].T for w in range(windows)]
    for k in range(0, slots, 2):
        found = []
        for q in (k, k + 1):
            name = partners_ref[i, q]
            safe = jnp.maximum(name, 0)
            slab = safe // blocks
            distance = lax.rem(slab // cols - r + HOP + rows, rows)
            place = jnp.where(name >= 0, distance * cols + lax.rem(slab, cols), 0)
            found.append((name >= 0, place, lax.rem(safe, blocks)))
        for w in range(windows):
            right = jnp.concatenate([cand_ref[s, w, b] for _, s, b in found], axis=1)
            tiles = jnp.dot(local[w], right, preferred_element_type=jnp.float32)
            for n, (present, _, _) in enumerate(found):
                tile = tiles[:, n * block_rows : (n + 1) * block_rows]
                out_ref[0, k + n, w] = jnp.where(present, tile, 0.0).astype(out_ref.dtype)


def on_device(rows, cols, bold, gm_index, partners):
    windows, frames, sx, sy, sz = bold.shape
    voxels = sx * sy * sz
    count = gm_index.shape[0]
    blocks, slots = partners.shape
    block_rows = count // blocks
    slabs = (2 * HOP + 1) * cols
    bf16, f32 = jnp.bfloat16, jnp.float32
    cand = pl.pallas_call(
        functools.partial(panel_kernel, rows),
        out_shape=jax.ShapeDtypeStruct((slabs, windows, blocks, frames, block_rows), bf16),
        in_specs=[pl.BlockSpec(memory_space=pltpu.VMEM)] * 2,
        out_specs=pl.BlockSpec(memory_space=pl.ANY),
        scratch_shapes=[
            pltpu.VMEM((windows, frames, sy, sz), bf16),
            pltpu.VMEM((windows, frames, sy, sz), bf16),
            pltpu.VMEM((voxels, count), bf16),
            pltpu.VMEM((sx, frames * sy, sz), f32),
            pltpu.VMEM((windows, sx, frames, sz), f32),
            pltpu.VMEM((windows, sx, frames, sz), f32),
            pltpu.VMEM((frames, voxels), bf16),
            pltpu.VMEM((windows, blocks, frames, block_rows), bf16),
            pltpu.SemaphoreType.DMA((windows, 2)),
            pltpu.SemaphoreType.DMA((windows, 2)),
            pltpu.SemaphoreType.DMA((windows,)),
            pltpu.SemaphoreType.DMA((windows,)),
            pltpu.SemaphoreType.DMA((windows,)),
            pltpu.SemaphoreType.DMA((windows, 9)),
            pltpu.SemaphoreType.DMA((windows, slabs)),
        ],
        compiler_params=pltpu.CompilerParams(
            collective_id=0, has_side_effects=True, vmem_limit_bytes=40 * 1024 * 1024
        ),
        name="panels",
    )(gm_index.reshape(1, count), bold)
    return pl.pallas_call(
        functools.partial(tile_kernel, rows, cols),
        out_shape=jax.ShapeDtypeStruct((blocks, slots, windows, block_rows, block_rows), bf16),
        grid_spec=pltpu.PrefetchScalarGridSpec(
            num_scalar_prefetch=1,
            grid=(blocks,),
            in_specs=[pl.BlockSpec(memory_space=pltpu.VMEM)],
            out_specs=pl.BlockSpec(
                (1, slots, windows, block_rows, block_rows), lambda i, names: (i, 0, 0, 0, 0)
            ),
        ),
        compiler_params=pltpu.CompilerParams(vmem_limit_bytes=40 * 1024 * 1024),
        name="tiles",
    )(partners, cand)


def solution(mesh):
    rows, cols = mesh.shape["row"], mesh.shape["col"]
    in_specs = (P("subj", None, "row", "col", None), P(("row", "col")), P(("row", "col"), None))
    out_specs = P(("row", "col"), None, "subj", None, None)
    return jax.shard_map(
        functools.partial(on_device, rows, cols),
        mesh=mesh,
        in_specs=in_specs,
        out_specs=out_specs,
        check_vma=False,
    )
```

time: 384 us -> 114 us (0.30)
  waiting for transfers between devices: 154 us -> 0 us
  local copies, waits for them, and re-layouts: 133 us -> 2.28 us
  Pallas kernels: 0 us -> 110 us
  other arithmetic: 57.5 us -> 0 us
  starting transfers between devices: 19 us -> 0 us
  between operations: 13.7 us -> 0.02 us
  matrix products: 5.71 us -> 0 us
    ppermute x8 -> x0, waiting for transfers between devices: 130 us -> none  [the longest x4 84.1 us: from_behind(): return lax.ppermute(value, axis, pairs)]
    pallas_call x0 -> x2, Pallas kernels: none -> 110 us  [the longest x1 102 us: on_device(): pl.pallas_call(functools.partial(panel_kernel, rows), out_shape=jax.Shape...]
    gather x11 -> x0, local copies, waits for them, and re-layouts: 83.3 us -> none  [the longest x8 78.3 us: block_tiles(): partner_rows = jnp.take(candidates, where_from, axis=0)]
    all_gather x1 -> x0, waiting for transfers between devices: 24.1 us -> none  [on_device(): collected = lax.all_gather(own_column, 'col', axis=1, tiled=True)]
    ppermute x8 -> x0, starting transfers between devices: 19 us -> none  [the longest x4 10.2 us: from_behind(): return lax.ppermute(value, axis, pairs)]
    select_n x18 -> x0, other arithmetic: 16.4 us -> none  [the longest x16 15.1 us: block_tiles(): partner_rows = jnp.take(candidates, where_from, axis=0)]
    add x3 -> x0, other arithmetic: 15.8 us -> none  [the longest x1 9.61 us: gaussian_blur(): side_weight * first[:, :, :, :-2] + centre_weight * first[:, :, :, 1:-1]]
    reshape x1 -> x0, local copies, waits for them, and re-layouts: 15.3 us -> none  [on_device(): collected.reshape((2 * HOP + 1) * col_count * block_count, block_rows, wi...]
  transfers between devices with their start and end apart: 9 -> 0, of which waited for: 6 -> 0; matrix products, arithmetic and copies ran while one was open for 3% -> 0% of each run, Pallas kernels for 0% -> 0%
where the time goes in v1:
time: 114 us; the launch traced here: 112 us
  Pallas kernels  110 us (96%)
  local copies, waits for them, and re-layouts  2.28 us (2%)
    pallas_call x1, Pallas kernels, on_device(): pl.pallas_call(functools.partial(panel_kernel, rows), out_shape=jax.Shape...  102 us
    pallas_call x1, Pallas kernels, on_device(): pl.pallas_call(functools.partial(tile_kernel, rows, cols), out_shape=jax....  7.26 us
    unnamed x6, local copies, waits for them, and re-layouts  2.28 us

profile of v1, /device:TPU:0, one launch (start us, length us, event | category | flops | bytes accessed | tf_op | source)
XLA Modules:
  0.0 111.8 jit_solution(1310811175577927147)
XLA Ops:
  0.0 0.0 copy-start
  0.0 1.6 %copy-done = bf16[2,256,2,8,128]{4,3,2,1,0:T(8,128)(2,1)S(1)} copy-done((bf16[2,256,2,8,128]{4,3,2,1,0:T(8,128)(2,1)S(1)}, bf16[2,256,2,8,128]{4,3,2,1,0:T(8,128)(2,1)}, u32[]{:S(2)}) %copy-start) | copy-done | bytes 2097176
  1.6 0.0 copy-start.1
  1.6 0.7 copy-done.1
  2.3 0.0 copy-start.2
  2.3 102.3 %panels.1.cand_ref = bf16[10,2,8,256,128]{4,3,2,1,0:T(8,128)(2,1)S(1)} custom-call(s32[1,1024]{1,0:T(1,128)S(1)} %bitcast.1, bf16[2,256,2,8,128]{4,3,2,1,0:T(8,128)(2,1)S(1)} %copy-done), custom_call_target="tpu_custom_call" | custom-call | tf_op jit(solution)/shard_map/panels/pallas_call | solution.py:319
  104.6 0.0 copy-done.2
  104.6 7.3 %tiles.1 = bf16[8,16,2,128,128]{4,3,2,1,0:T(8,128)(2,1)} custom-call(s32[8,16]{1,0:T(8,128)S(1)} %copy-done.2, bf16[10,2,8,256,128]{4,3,2,1,0:T(8,128)(2,1)S(1)} %panels.1.cand_ref), custom_call_target="tpu_custom_call" | custom-call | tf_op jit(solution)/shard_map/tiles/pallas_call | solution.py:346
Async XLA Ops:
  0.0 1.6 %copy-start = (bf16[2,256,2,8,128]{4,3,2,1,0:T(8,128)(2,1)S(1)}, bf16[2,256,2,8,128]{4,3,2,1,0:T(8,128)(2,1)}, u32[]{:S(2)}) copy-start(bf16[2,256,2,8,128]{4,3,2,1,0:T(8,128)(2,1)} %bold_ref.1) | copy-start | bytes 6291460
  1.6 0.7 copy-start.1
  2.3 102.3 %copy-start.2 = (s32[8,16]{1,0:T(8,128)S(1)}, s32[8,16]{1,0:T(8,128)}, u32[]{:S(2)}) copy-start(s32[8,16]{1,0:T(8,128)} %partners_ref.1) | copy-start | bytes 1540

commit v2 on v1

--- a/solution.py
+++ b/solution.py
@@ -164,6 +164,8 @@
         def _():
             halo_down(w).wait_recv()
 
+        if w > 0:
+            to_pair(w - 1).start()
         chunk = 32
 
         def filter_x(step, carry):
@@ -236,7 +238,8 @@
 
         to_up2(w).start()
         to_down2(w).start()
-        to_pair(w).start()
+        if w > 0:
+            to_pair(w).start()
         to_other(w).start()
         own(w).start()
 
@@ -246,17 +249,35 @@
         2 * (4 * odd) + c,
         2 * (1 + 2 * odd) + c,
     )
-    for w in range(windows):
-        arrived(w, order[0])
-        across(w, 0, order[0]).start()
-        arrived(w, order[1])
-        relay(w).start()
-        across(w, 1, order[1]).start()
-        arrived(w, order[2])
-        across(w, 2, order[2]).start()
-    for w in range(windows):
-        arrived(w, order[3])
-        across(w, 3, order[3]).start()
+    inside = r + (rows - 2 * r - 1) * odd < rows - 2
+
+    def relay_far(w):
+        target = up2 + (down2 - up2) * odd
+        return send(w, cand_ref.at[order[0], w], 2 * (1 + 2 * odd) + c, 4, {"row": target})
+
+    def pass_on(w, which):
+        arrived(w, order[which])
+        across(w, which, order[which]).start()
+
+    pass_on(0, 1)
+    relay(0).start()
+    pass_on(0, 2)
+    pass_on(0, 0)
+    pass_on(1, 0)
+
+    @pl.when(inside)
+    def _():
+        relay_far(1).start()
+
+    pass_on(1, 1)
+
+    @pl.when(jnp.logical_not(inside))
+    def _():
+        relay(1).start()
+
+    pass_on(1, 2)
+    pass_on(0, 3)
+    pass_on(1, 3)
 
     for w in range(windows):
         for slot in range(2 * HOP + 1):
@@ -277,20 +298,30 @@
         to_up2(w).wait_send()
         to_down2(w).wait_send()
         to_pair(w).wait_send()
-        relay(w).wait_send()
+        if w == 0:
+            relay(w).wait_send()
+        else:
+
+            @pl.when(inside)
+            def _():
+                relay_far(w).wait_send()
+
+            @pl.when(jnp.logical_not(inside))
+            def _():
+                relay(w).wait_send()
+
         for which in range(4):
             across(w, which, order[which]).wait_send()
 
 
 def tile_kernel(rows, cols, partners_ref, cand_ref, out_ref):
-    i = pl.program_id(0)
+    i = pl.program_id(1)
     blocks = cand_ref.shape[2]
     block_rows = cand_ref.shape[4]
-    windows = cand_ref.shape[1]
     slots = out_ref.shape[1]
     r = lax.axis_index("row")
     c = lax.axis_index("col")
-    local = [cand_ref[HOP * cols + c, w, i].T for w in range(windows)]
+    local = cand_ref[HOP * cols + c, 0, i].T
     for k in range(0, slots, 2):
         found = []
         for q in (k, k + 1):
@@ -300,12 +331,11 @@
             distance = lax.rem(slab // cols - r + HOP + rows, rows)
             place = jnp.where(name >= 0, distance * cols + lax.rem(slab, cols), 0)
             found.append((name >= 0, place, lax.rem(safe, blocks)))
-        for w in range(windows):
-            right = jnp.concatenate([cand_ref[s, w, b] for _, s, b in found], axis=1)
-            tiles = jnp.dot(local[w], right, preferred_element_type=jnp.float32)
-            for n, (present, _, _) in enumerate(found):
-                tile = tiles[:, n * block_rows : (n + 1) * block_rows]
-                out_ref[0, k + n, w] = jnp.where(present, tile, 0.0).astype(out_ref.dtype)
+        right = jnp.concatenate([cand_ref[s, 0, b] for _, s, b in found], axis=1)
+        tiles = jnp.dot(local, right, preferred_element_type=jnp.float32)
+        for n, (present, _, _) in enumerate(found):
+            tile = tiles[:, n * block_rows : (n + 1) * block_rows]
+            out_ref[0, k + n, 0] = jnp.where(present, tile, 0.0).astype(out_ref.dtype)
 
 
 def on_device(rows, cols, bold, gm_index, partners):
@@ -348,10 +378,14 @@
         out_shape=jax.ShapeDtypeStruct((blocks, slots, windows, block_rows, block_rows), bf16),
         grid_spec=pltpu.PrefetchScalarGridSpec(
             num_scalar_prefetch=1,
-            grid=(blocks,),
-            in_specs=[pl.BlockSpec(memory_space=pltpu.VMEM)],
+            grid=(windows, blocks),
+            in_specs=[
+                pl.BlockSpec(
+                    (slabs, 1, blocks, frames, block_rows), lambda w, i, names: (0, w, 0, 0, 0)
+                )
+            ],
             out_specs=pl.BlockSpec(
-                (1, slots, windows, block_rows, block_rows), lambda i, names: (i, 0, 0, 0, 0)
+                (1, slots, 1, block_rows, block_rows), lambda w, i, names: (i, 0, w, 0, 0)
             ),
         ),
         compiler_params=pltpu.CompilerParams(vmem_limit_bytes=40 * 1024 * 1024),

time: 114 us -> 113 us (level); the launches traced: 112 us -> 113 us
    pallas_call x1, Pallas kernels: 7.26 us -> 11.6 us  [on_device(): pl.pallas_call(functools.partial(tile_kernel, rows, cols), out_shape=jax....]
    pallas_call x1, Pallas kernels: 102 us -> 99.2 us  [on_device(): pl.pallas_call(functools.partial(panel_kernel, rows), out_shape=jax.Shape...]
where the time goes in v2:
time: 113 us
  Pallas kernels  111 us (98%)
  local copies, waits for them, and re-layouts  2.28 us (2%)
    pallas_call x1, Pallas kernels, on_device(): pl.pallas_call(functools.partial(panel_kernel, rows), out_shape=jax.Shape...  99.2 us
    pallas_call x1, Pallas kernels, on_device(): pl.pallas_call(functools.partial(tile_kernel, rows, cols), out_shape=jax....  11.6 us
    unnamed x6, local copies, waits for them, and re-layouts  2.28 us

profile of v2, /device:TPU:0, one launch (start us, length us, event | category | flops | bytes accessed | tf_op | source)
XLA Modules:
  0.0 113.1 jit_solution(8532399362500823602)
XLA Ops:
  0.0 0.0 copy-start
  0.0 1.6 %copy-done = bf16[2,256,2,8,128]{4,3,2,1,0:T(8,128)(2,1)S(1)} copy-done((bf16[2,256,2,8,128]{4,3,2,1,0:T(8,128)(2,1)S(1)}, bf16[2,256,2,8,128]{4,3,2,1,0:T(8,128)(2,1)}, u32[]{:S(2)}) %copy-start) | copy-done | bytes 2097176
  1.6 0.0 copy-start.1
  1.6 0.7 copy-done.1
  2.3 0.0 copy-start.2
  2.3 99.2 %panels.1.cand_ref = bf16[10,2,8,256,128]{4,3,2,1,0:T(8,128)(2,1)S(1)} custom-call(s32[1,1024]{1,0:T(1,128)S(1)} %bitcast.1, bf16[2,256,2,8,128]{4,3,2,1,0:T(8,128)(2,1)S(1)} %copy-done), custom_call_target="tpu_custom_call" | custom-call | tf_op jit(solution)/shard_map/panels/pallas_call | solution.py:349
  101.5 0.0 copy-done.2
  101.5 11.6 %tiles.1 = bf16[8,16,2,128,128]{4,3,2,1,0:T(8,128)(2,1)} custom-call(s32[8,16]{1,0:T(8,128)S(1)} %copy-done.2, bf16[10,2,8,256,128]{4,3,2,1,0:T(8,128)(2,1)S(1)} %panels.1.cand_ref), custom_call_target="tpu_custom_call" | custom-call | tf_op jit(solution)/shard_map/tiles/pallas_call | solution.py:376
Async XLA Ops:
  0.0 1.6 %copy-start = (bf16[2,256,2,8,128]{4,3,2,1,0:T(8,128)(2,1)S(1)}, bf16[2,256,2,8,128]{4,3,2,1,0:T(8,128)(2,1)}, u32[]{:S(2)}) copy-start(bf16[2,256,2,8,128]{4,3,2,1,0:T(8,128)(2,1)} %bold_ref.1) | copy-start | bytes 6291460
  1.6 0.7 copy-start.1
  2.3 99.3 %copy-start.2 = (s32[8,16]{1,0:T(8,128)S(1)}, s32[8,16]{1,0:T(8,128)}, u32[]{:S(2)}) copy-start(s32[8,16]{1,0:T(8,128)} %partners_ref.1) | copy-start | bytes 1540

commit v3 on v2

--- a/solution.py
+++ b/solution.py
@@ -24,8 +24,8 @@
     gm_ref,
     bold_ref,
     cand_ref,
-    halo_lo,
-    halo_hi,
+    halo,
+    halo_via,
     pick,
     xf,
     face_out,
@@ -60,43 +60,44 @@
         pl.semaphore_signal(barrier, inc=1, device_id={"row": target}, device_id_type=MESH)
     pl.semaphore_wait(barrier, 5)
 
-    def halo_up(w):
+    far = up2 * odd + down2 * (1 - odd)
+    inside = r + (rows - 2 * r - 1) * odd < rows - 2
+    far_side = r + (rows - 2 * r - 1) * odd > 0
+
+    def halo_copy(w, src, dst, sem, target):
         return pltpu.make_async_remote_copy(
-            src_ref=bold_ref.at[w, :, sx - 1],
-            dst_ref=halo_lo.at[w],
-            send_sem=halo_send.at[w, 0],
-            recv_sem=halo_recv.at[w, 0],
-            device_id={"row": up1},
+            src_ref=src,
+            dst_ref=dst,
+            send_sem=halo_send.at[w, sem],
+            recv_sem=halo_recv.at[w, sem],
+            device_id={"row": target},
             device_id_type=MESH,
         )
 
-    def halo_down(w):
-        return pltpu.make_async_remote_copy(
-            src_ref=bold_ref.at[w, :, 0],
-            dst_ref=halo_hi.at[w],
-            send_sem=halo_send.at[w, 1],
-            recv_sem=halo_recv.at[w, 1],
-            device_id={"row": down1},
-            device_id_type=MESH,
-        )
+    def halo_far(w):
+        return halo_copy(w, bold_ref.at[w, :, (sx - 1) * odd], halo_via.at[w], 0, far)
+
+    def halo_pair(w):
+        return halo_copy(w, bold_ref.at[w, :, (sx - 1) * (1 - odd)], halo.at[odd, w], 1, pair)
+
+    def halo_relay(w):
+        return halo_copy(w, halo_via.at[w], halo.at[1 - odd, w], 2, pair)
 
     for w in range(windows):
 
-        @pl.when(r < rows - 1)
+        @pl.when(far_side)
         def _():
-            halo_up(w).start()
-
-        @pl.when(r > 0)
-        def _():
-            halo_down(w).start()
+            halo_far(w).start()
+
+    halo_pair(0).start()
 
     @pl.when(r == 0)
     def _():
-        halo_lo[...] = jnp.zeros_like(halo_lo)
+        halo[0] = jnp.zeros_like(halo[0])
 
     @pl.when(r == rows - 1)
     def _():
-        halo_hi[...] = jnp.zeros_like(halo_hi)
+        halo[1] = jnp.zeros_like(halo[1])
 
     gm = gm_ref[...]
 
@@ -107,6 +108,16 @@
         return carry
 
     lax.fori_loop(0, voxels // sz, fill, 0)
+
+    for w in range(windows):
+
+        @pl.when(inside)
+        def _():
+            halo_far(w).wait_recv()
+            halo_relay(w).start()
+
+        if w + 1 < windows:
+            halo_pair(w + 1).start()
 
     def send(w, src, slot, sem, target):
         return pltpu.make_async_remote_copy(
@@ -156,13 +167,11 @@
 
     for w in range(windows):
 
-        @pl.when(r > 0)
+        halo_pair(w).wait_recv()
+
+        @pl.when(far_side)
         def _():
-            halo_up(w).wait_recv()
-
-        @pl.when(r < rows - 1)
-        def _():
-            halo_down(w).wait_recv()
+            halo_relay(w).wait_recv()
 
         if w > 0:
             to_pair(w - 1).start()
@@ -171,10 +180,10 @@
         def filter_x(step, carry):
             at = step * chunk
             here = pl.ds(at, chunk)
-            low = halo_lo[w, here].astype(jnp.float32)
+            low = halo[0, w, here].astype(jnp.float32)
             first = bold_ref[w, here, 0].astype(jnp.float32)
             second = bold_ref[w, here, 1].astype(jnp.float32)
-            high = halo_hi[w, here].astype(jnp.float32)
+            high = halo[1, w, here].astype(jnp.float32)
             flat = pl.ds(pl.multiple_of(at * sy, sy), chunk * sy)
             xf[0, flat, :] = three(low, first, second).reshape(chunk * sy, sz)
             xf[1, flat, :] = three(first, second, high).reshape(chunk * sy, sz)
@@ -249,7 +258,6 @@
         2 * (4 * odd) + c,
         2 * (1 + 2 * odd) + c,
     )
-    inside = r + (rows - 2 * r - 1) * odd < rows - 2
 
     def relay_far(w):
         target = up2 + (down2 - up2) * odd
@@ -285,13 +293,15 @@
 
     for w in range(windows):
 
-        @pl.when(r < rows - 1)
+        halo_pair(w).wait_send()
+
+        @pl.when(far_side)
         def _():
-            halo_up(w).wait_send()
-
-        @pl.when(r > 0)
+            halo_far(w).wait_send()
+
+        @pl.when(inside)
         def _():
-            halo_down(w).wait_send()
+            halo_relay(w).wait_send()
 
         own(w).wait()
         to_other(w).wait_send()
@@ -315,13 +325,14 @@
 
 
 def tile_kernel(rows, cols, partners_ref, cand_ref, out_ref):
-    i = pl.program_id(1)
+    i = pl.program_id(0)
     blocks = cand_ref.shape[2]
     block_rows = cand_ref.shape[4]
+    windows = cand_ref.shape[1]
     slots = out_ref.shape[1]
     r = lax.axis_index("row")
     c = lax.axis_index("col")
-    local = cand_ref[HOP * cols + c, 0, i].T
+    local = [cand_ref[HOP * cols + c, w, i].T for w in range(windows)]
     for k in range(0, slots, 2):
         found = []
         for q in (k, k + 1):
@@ -331,11 +342,12 @@
             distance = lax.rem(slab // cols - r + HOP + rows, rows)
             place = jnp.where(name >= 0, distance * cols + lax.rem(slab, cols), 0)
             found.append((name >= 0, place, lax.rem(safe, blocks)))
-        right = jnp.concatenate([cand_ref[s, 0, b] for _, s, b in found], axis=1)
-        tiles = jnp.dot(local, right, preferred_element_type=jnp.float32)
-        for n, (present, _, _) in enumerate(found):
-            tile = tiles[:, n * block_rows : (n + 1) * block_rows]
-            out_ref[0, k + n, 0] = jnp.where(present, tile, 0.0).astype(out_ref.dtype)
+        for w in range(windows):
+            right = jnp.concatenate([cand_ref[s, w, b] for _, s, b in found], axis=1)
+            tiles = jnp.dot(local[w], right, preferred_element_type=jnp.float32)
+            for n, (present, _, _) in enumerate(found):
+                tile = tiles[:, n * block_rows : (n + 1) * block_rows]
+                out_ref[0, k + n, w] = jnp.where(present, tile, 0.0).astype(out_ref.dtype)
 
 
 def on_device(rows, cols, bold, gm_index, partners):
@@ -352,7 +364,7 @@
         in_specs=[pl.BlockSpec(memory_space=pltpu.VMEM)] * 2,
         out_specs=pl.BlockSpec(memory_space=pl.ANY),
         scratch_shapes=[
-            pltpu.VMEM((windows, frames, sy, sz), bf16),
+            pltpu.VMEM((2, windows, frames, sy, sz), bf16),
             pltpu.VMEM((windows, frames, sy, sz), bf16),
             pltpu.VMEM((voxels, count), bf16),
             pltpu.VMEM((sx, frames * sy, sz), f32),
@@ -360,8 +372,8 @@
             pltpu.VMEM((windows, sx, frames, sz), f32),
             pltpu.VMEM((frames, voxels), bf16),
             pltpu.VMEM((windows, blocks, frames, block_rows), bf16),
-            pltpu.SemaphoreType.DMA((windows, 2)),
-            pltpu.SemaphoreType.DMA((windows, 2)),
+            pltpu.SemaphoreType.DMA((windows, 3)),
+            pltpu.SemaphoreType.DMA((windows, 3)),
             pltpu.SemaphoreType.DMA((windows,)),
             pltpu.SemaphoreType.DMA((windows,)),
             pltpu.SemaphoreType.DMA((windows,)),
@@ -378,14 +390,10 @@
         out_shape=jax.ShapeDtypeStruct((blocks, slots, windows, block_rows, block_rows), bf16),
         grid_spec=pltpu.PrefetchScalarGridSpec(
             num_scalar_prefetch=1,
-            grid=(windows, blocks),
-            in_specs=[
-                pl.BlockSpec(
-                    (slabs, 1, blocks, frames, block_rows), lambda w, i, names: (0, w, 0, 0, 0)
-                )
-            ],
+            grid=(blocks,),
+            in_specs=[pl.BlockSpec(memory_space=pltpu.VMEM)],
             out_specs=pl.BlockSpec(
-                (1, slots, 1, block_rows, block_rows), lambda w, i, names: (i, 0, w, 0, 0)
+                (1, slots, windows, block_rows, block_rows), lambda i, names: (i, 0, 0, 0, 0)
             ),
         ),
         compiler_params=pltpu.CompilerParams(vmem_limit_bytes=40 * 1024 * 1024),

time: 113 us -> 110 us (0.973)
  Pallas kernels: 111 us -> 107 us
    pallas_call x1, Pallas kernels: 11.6 us -> 7.27 us  [on_device(): pl.pallas_call(functools.partial(tile_kernel, rows, cols), out_shape=jax....]
where the time goes in v3:
time: 110 us
  Pallas kernels  107 us (97%)
  local copies, waits for them, and re-layouts  2.28 us (2%)
    pallas_call x1, Pallas kernels, on_device(): pl.pallas_call(functools.partial(panel_kernel, rows), out_shape=jax.Shape...  100 us
    pallas_call x1, Pallas kernels, on_device(): pl.pallas_call(functools.partial(tile_kernel, rows, cols), out_shape=jax....  7.27 us
    unnamed x6, local copies, waits for them, and re-layouts  2.28 us

profile of v3, /device:TPU:0, one launch (start us, length us, event | category | flops | bytes accessed | tf_op | source)
XLA Modules:
  0.0 109.6 jit_solution(2141750029211817533)
XLA Ops:
  0.0 0.0 copy-start
  0.0 1.6 %copy-done = bf16[2,256,2,8,128]{4,3,2,1,0:T(8,128)(2,1)S(1)} copy-done((bf16[2,256,2,8,128]{4,3,2,1,0:T(8,128)(2,1)S(1)}, bf16[2,256,2,8,128]{4,3,2,1,0:T(8,128)(2,1)}, u32[]{:S(2)}) %copy-start) | copy-done | bytes 2097176
  1.6 0.0 copy-start.1
  1.6 0.7 copy-done.1
  2.3 0.0 copy-start.2
  2.3 100.1 %panels.1.cand_ref = bf16[10,2,8,256,128]{4,3,2,1,0:T(8,128)(2,1)S(1)} custom-call(s32[1,1024]{1,0:T(1,128)S(1)} %bitcast.1, bf16[2,256,2,8,128]{4,3,2,1,0:T(8,128)(2,1)S(1)} %copy-done), custom_call_target="tpu_custom_call" | custom-call | tf_op jit(solution)/shard_map/panels/pallas_call | solution.py:361
  102.4 0.0 copy-done.2
  102.4 7.3 %tiles.1 = bf16[8,16,2,128,128]{4,3,2,1,0:T(8,128)(2,1)} custom-call(s32[8,16]{1,0:T(8,128)S(1)} %copy-done.2, bf16[10,2,8,256,128]{4,3,2,1,0:T(8,128)(2,1)S(1)} %panels.1.cand_ref), custom_call_target="tpu_custom_call" | custom-call | tf_op jit(solution)/shard_map/tiles/pallas_call | solution.py:388
Async XLA Ops:
  0.0 1.6 %copy-start = (bf16[2,256,2,8,128]{4,3,2,1,0:T(8,128)(2,1)S(1)}, bf16[2,256,2,8,128]{4,3,2,1,0:T(8,128)(2,1)}, u32[]{:S(2)}) copy-start(bf16[2,256,2,8,128]{4,3,2,1,0:T(8,128)(2,1)} %bold_ref.1) | copy-start | bytes 6291460
  1.6 0.7 copy-start.1
  2.3 100.1 %copy-start.2 = (s32[8,16]{1,0:T(8,128)S(1)}, s32[8,16]{1,0:T(8,128)}, u32[]{:S(2)}) copy-start(s32[8,16]{1,0:T(8,128)} %partners_ref.1) | copy-start | bytes 1540

commit v4 on v3

--- a/solution.py
+++ b/solution.py
@@ -24,6 +24,7 @@
     gm_ref,
     bold_ref,
     cand_ref,
+    held,
     halo,
     halo_via,
     pick,
@@ -32,6 +33,7 @@
     face_in,
     scored,
     panel,
+    load_sem,
     halo_send,
     halo_recv,
     face_send,
@@ -54,6 +56,8 @@
     down2 = lax.rem(r + rows - 2, rows)
     other = {"col": 1 - c}
 
+    load = pltpu.make_async_copy(bold_ref, held, load_sem)
+    load.start()
     barrier = pltpu.get_barrier_semaphore()
     pl.semaphore_signal(barrier, inc=1, device_id=other, device_id_type=MESH)
     for target in (up1, down1, up2, down2):
@@ -109,15 +113,16 @@
 
     lax.fori_loop(0, voxels // sz, fill, 0)
 
-    for w in range(windows):
-
+    def pass_halo(w):
         @pl.when(inside)
         def _():
             halo_far(w).wait_recv()
             halo_relay(w).start()
 
-        if w + 1 < windows:
-            halo_pair(w + 1).start()
+    pass_halo(0)
+    for w in range(1, windows):
+        halo_pair(w).start()
+    load.wait()
 
     def send(w, src, slot, sem, target):
         return pltpu.make_async_remote_copy(
@@ -167,6 +172,8 @@
 
     for w in range(windows):
 
+        if w > 0:
+            pass_halo(w)
         halo_pair(w).wait_recv()
 
         @pl.when(far_side)
@@ -181,8 +188,8 @@
             at = step * chunk
             here = pl.ds(at, chunk)
             low = halo[0, w, here].astype(jnp.float32)
-            first = bold_ref[w, here, 0].astype(jnp.float32)
-            second = bold_ref[w, here, 1].astype(jnp.float32)
+            first = held[w, here, 0].astype(jnp.float32)
+            second = held[w, here, 1].astype(jnp.float32)
             high = halo[1, w, here].astype(jnp.float32)
             flat = pl.ds(pl.multiple_of(at * sy, sy), chunk * sy)
             xf[0, flat, :] = three(low, first, second).reshape(chunk * sy, sz)
@@ -361,9 +368,13 @@
     cand = pl.pallas_call(
         functools.partial(panel_kernel, rows),
         out_shape=jax.ShapeDtypeStruct((slabs, windows, blocks, frames, block_rows), bf16),
-        in_specs=[pl.BlockSpec(memory_space=pltpu.VMEM)] * 2,
+        in_specs=[
+            pl.BlockSpec(memory_space=pltpu.VMEM),
+            pl.BlockSpec(memory_space=pl.ANY),
+        ],
         out_specs=pl.BlockSpec(memory_space=pl.ANY),
         scratch_shapes=[
+            pltpu.VMEM(bold.shape, bf16),
             pltpu.VMEM((2, windows, frames, sy, sz), bf16),
             pltpu.VMEM((windows, frames, sy, sz), bf16),
             pltpu.VMEM((voxels, count), bf16),
@@ -372,6 +383,7 @@
             pltpu.VMEM((windows, sx, frames, sz), f32),
             pltpu.VMEM((frames, voxels), bf16),
             pltpu.VMEM((windows, blocks, frames, block_rows), bf16),
+            pltpu.SemaphoreType.DMA,
             pltpu.SemaphoreType.DMA((windows, 3)),
             pltpu.SemaphoreType.DMA((windows, 3)),
             pltpu.SemaphoreType.DMA((windows,)),

time: 110 us -> 110 us (level)
  no operation moved by 1% of the time
where the time goes in v4:
time: 110 us
  Pallas kernels  107 us (97%)
  local copies, waits for them, and re-layouts  2.28 us (2%)
    pallas_call x1, Pallas kernels, on_device(): pl.pallas_call(functools.partial(panel_kernel, rows), out_shape=jax.Shape...  100 us
    pallas_call x1, Pallas kernels, on_device(): pl.pallas_call(functools.partial(tile_kernel, rows, cols), out_shape=jax....  7.27 us
    unnamed x6, local copies, waits for them, and re-layouts  2.28 us

profile of v4, /device:TPU:0, one launch (start us, length us, event | category | flops | bytes accessed | tf_op | source)
XLA Modules:
  0.0 109.8 jit_solution(12816027958434633792)
XLA Ops:
  0.0 0.0 copy-start
  0.0 1.6 %copy-done = bf16[2,256,2,8,128]{4,3,2,1,0:T(8,128)(2,1)S(1)} copy-done((bf16[2,256,2,8,128]{4,3,2,1,0:T(8,128)(2,1)S(1)}, bf16[2,256,2,8,128]{4,3,2,1,0:T(8,128)(2,1)}, u32[]{:S(2)}) %copy-start) | copy-done | bytes 2097176
  1.6 0.0 copy-start.1
  1.6 0.7 copy-done.1
  2.3 0.0 copy-start.2
  2.3 100.2 %panels.1.cand_ref = bf16[10,2,8,256,128]{4,3,2,1,0:T(8,128)(2,1)S(1)} custom-call(s32[1,1024]{1,0:T(1,128)S(1)} %bitcast.1, bf16[2,256,2,8,128]{4,3,2,1,0:T(8,128)(2,1)S(1)} %copy-done), custom_call_target="tpu_custom_call" | custom-call | tf_op jit(solution)/shard_map/panels/pallas_call | solution.py:368
  102.5 0.0 copy-done.2
  102.5 7.3 %tiles.1 = bf16[8,16,2,128,128]{4,3,2,1,0:T(8,128)(2,1)} custom-call(s32[8,16]{1,0:T(8,128)S(1)} %copy-done.2, bf16[10,2,8,256,128]{4,3,2,1,0:T(8,128)(2,1)S(1)} %panels.1.cand_ref), custom_call_target="tpu_custom_call" | custom-call | tf_op jit(solution)/shard_map/tiles/pallas_call | solution.py:400
Async XLA Ops:
  0.0 1.6 %copy-start = (bf16[2,256,2,8,128]{4,3,2,1,0:T(8,128)(2,1)S(1)}, bf16[2,256,2,8,128]{4,3,2,1,0:T(8,128)(2,1)}, u32[]{:S(2)}) copy-start(bf16[2,256,2,8,128]{4,3,2,1,0:T(8,128)(2,1)} %bold_ref.1) | copy-start | bytes 6291460
  1.6 0.7 copy-start.1
  2.3 100.2 %copy-start.2 = (s32[8,16]{1,0:T(8,128)S(1)}, s32[8,16]{1,0:T(8,128)}, u32[]{:S(2)}) copy-start(s32[8,16]{1,0:T(8,128)} %partners_ref.1) | copy-start | bytes 1540
